TPU v7x, 256 devices: a whole 4x4x8 slice. The times are simulated.
256 devices in a mesh: row: 32 (over x, z), col: 8 (over y, core).
Axes of the slice: x: 4, y: 4, z: 8, core: 2. Of those that a mesh axis runs over, the one named last changes fastest.
Arguments:
- mom_a: float32 [1536, 12288], P('row', 'col'), may hold values from -6 to 6
- grad_a: float32 [1536, 12288], P('row', 'col'), may hold values from -6 to 6
- basis_a: float32 [512, 12288], P('row', 'col'), may hold values from -0.0546875 to 0.0546875
- mom_b: float32 [7168, 1536], P('row', 'col'), may hold values from -6 to 6
- grad_b: float32 [7168, 1536], P('row', 'col'), may hold values from -6 to 6
- basis_b: float32 [512, 1536], P('row', 'col'), may hold values from -0.15625 to 0.15625
Outputs:
- new_mom_a: float32 [1536, 12288], P('row', 'col')
- update_a: bfloat16 [1536, 12288], P('row', 'col')
- new_basis_a: float32 [512, 12288], P('row', 'col')
- new_mom_b: float32 [7168, 1536], P('row', 'col')
- update_b: bfloat16 [7168, 1536], P('row', 'col')
- new_basis_b: float32 [512, 1536], P('row', 'col')
All inputs are finite; a program needn't handle non-finite values.
Results may differ from a plain program's by a relative error of at most 0.0049.
Values sent between devices are 32-bit elements; how exact they have to be, the bound alone decides.
No kernel may reach another device: no remote copies, remote signals or barrier semaphores. Data moves between devices by JAX's collectives and lax.ppermute only.
A program may use at most 64 MiB of HBM per device.

v0:
```python
import math
import jax
import jax.numpy as jnp
from jax import lax
from jax.sharding import PartitionSpec as P

MU = 0.95
EPS = 1e-06


def sent_to_all(array, axis):
    size = lax.axis_size(axis)
    return lax.all_to_all(
        jnp.broadcast_to(array[None], (size, *array.shape)), axis, 0, 0, tiled=True
    )


def over_copies(array, axis):
    everything = sent_to_all(array, axis)
    return jnp.sum(everything, axis=0)


def split_up(array, dim, size):
    before, after = (array.shape[:dim], array.shape[dim + 1 :])
    return jnp.moveaxis(array.reshape(*before, size, -1, *after), dim, 0)


def summed_on_arrival(array, axis, dim):
    size = lax.axis_size(axis)
    parts = lax.all_to_all(split_up(array, dim, size), axis, 0, 0, tiled=True)
    return jnp.sum(parts, axis=0)


def in_one_piece(arrays, axis, dim, along):
    widths = [a.shape[along] for a in arrays]
    both = jnp.concatenate(arrays, axis=along)
    whole = lax.all_gather(both, axis, axis=dim, tiled=True)
    return tuple(jnp.split(whole, [sum(widths[:k]) for k in range(1, len(widths))], axis=along))


def together(arrays, axis):
    ends = [0]
    for a in arrays:
        ends.append(ends[-1] + a.size)
    so_far = lax.psum(jnp.concatenate([a.ravel() for a in arrays]), axis)
    return tuple((so_far[b:e].reshape(a.shape) for a, b, e in zip(arrays, ends, ends[1:])))


def project(buffer, basis):
    partial_proj = jnp.dot(
        buffer,
        lax.all_gather(basis, "row", axis=0, tiled=True).T,
        precision=lax.Precision.HIGHEST,
        preferred_element_type=jnp.float32,
    )
    return over_copies(partial_proj, "col")


def local_gram(proj):
    return jnp.dot(
        proj.T, proj, precision=lax.Precision.HIGHEST, preferred_element_type=jnp.float32
    )


def finish(buffer, proj, gram):
    highest = lax.Precision.HIGHEST
    lower = jnp.linalg.cholesky(gram)
    ortho = lax.linalg.triangular_solve(lower, proj, left_side=False, lower=True, transpose_a=True)
    rank = ortho.shape[1]
    share = summed_on_arrival(
        jnp.dot(ortho.T, buffer, precision=highest, preferred_element_type=jnp.float32), "row", 0
    )
    squares = over_copies(jnp.sum(share * share, axis=1, keepdims=True), "col")
    norms = jnp.sqrt(squares + EPS)
    own_basis = share / norms
    full_basis, full_norms = in_one_piece((own_basis, norms), "row", 0, 1)
    trans = full_basis * full_norms
    new_mom = buffer - (1.0 - MU) * jnp.dot(
        ortho, trans, precision=highest, preferred_element_type=jnp.float32
    )
    total_rows = buffer.shape[0] * lax.axis_size("row")
    total_cols = buffer.shape[1] * lax.axis_size("col")
    scale = math.sqrt(total_rows * total_cols / rank)
    update = (
        jnp.dot(ortho, full_basis, precision=highest, preferred_element_type=jnp.float32) * scale
    ).astype(jnp.bfloat16)
    return (new_mom, update, own_basis)


def shards(mom_a, grad_a, basis_a, mom_b, grad_b, basis_b):
    buffers = [MU * mom_a + grad_a, MU * mom_b + grad_b]
    projs = [project(buffers[0], basis_a), project(buffers[1], basis_b)]
    grams = together((local_gram(projs[0]), local_gram(projs[1])), "row")
    first = finish(buffers[0], projs[0], grams[0])
    second = finish(buffers[1], projs[1], grams[1])
    return (first[0], first[1], first[2], second[0], second[1], second[2])


def solution(mesh):
    return jax.shard_map(
        shards,
        mesh=mesh,
        in_specs=(
            P("row", "col"),
            P("row", "col"),
            P("row", "col"),
            P("row", "col"),
            P("row", "col"),
            P("row", "col"),
        ),
        out_specs=(
            P("row", "col"),
            P("row", "col"),
            P("row", "col"),
            P("row", "col"),
            P("row", "col"),
            P("row", "col"),
        ),
        check_vma=False,
    )
```

profile of v0, /device:TPU:8, one launch (start us, length us, event | category | flops | bytes accessed | tf_op | source)
XLA Modules:
  0.0 711.3 jit_solution(5581359570950233791)
XLA Ops:
  7.9 52.6 %all_gather.13 = f32[512,192]{1,0:T(8,128)S(1)} all-gather(f32[16,192]{1,0:T(8,128)} %param.12), channel_id=1, replica_groups=mesh['row'=32,'col'=8] {'row'}, dimensions={0}, use_global_device_ids=true | all-gather | bytes 405504 | tf_op jit(solution)/shard_map/all_gather | solution.py:52
  64.9 5.0 all-to-all-start.1
  69.8 23.7 %all-gather.3.cloned.1.call-done = f32[512,1536]{1,0:T(8,128)} async-done(((f32[16,1536]{1,0:T(8,128)}), f32[512,1536]{1,0:T(8,128)}) %all-gather.3.cloned.1.call-update) | async-done | bytes 3145744 | tf_op jit(solution)/shard_map/all_gather | solution.py:52
  93.5 4.9 fusion.95
  98.4 14.1 %all-to-all-done.1 = f32[8,224,512]{2,1,0:T(8,128)} async-done(((f32[8,224,512]{2,1,0:T(8,128)}), f32[8,224,512]{2,1,0:T(8,128)}, u32[]{:S(2)}, u32[]{:S(2)}) %all-to-all-start.1) | async-done | bytes 3670048 | tf_op jit(solution)/shard_map/all_to_all | solution.py:13
  113.5 4.9 all-to-all-start
  122.9 7.3 %all-to-all-done = f32[8,48,512]{2,1,0:T(8,128)S(1)} async-done(((f32[8,48,512]{2,1,0:T(8,128)}), f32[8,48,512]{2,1,0:T(8,128)S(1)}, u32[]{:S(2)}, u32[]{:S(2)}) %all-to-all-start) | async-done | bytes 786464 | tf_op jit(solution)/shard_map/all_to_all | solution.py:13
  133.0 151.3 %all-reduce.3.cloned.1.call-done = f32[524288]{0:T(1024)} async-done(((f32[524288]{0:T(1024)}), f32[524288]{0:T(1024)}) %all-reduce.3.cloned.1.call-update) | async-done | bytes 2097168 | tf_op jit(solution)/shard_map/psum | solution.py:45
  287.7 11.7 %cholesky.286 = f32[128,128]{1,0:T(8,128)S(1)} custom-call(f32[128,128]{1,0:T(8,128)S(1)} %cholesky.426), custom_call_target="Cholesky" | custom-call | tf_op jit(solution)/shard_map/jit(cholesky)/cholesky | solution.py:67
  299.5 9.8 %custom-call.31 = f32[1,128,128]{1,2,0:T(8,128)S(1)} custom-call(f32[1,128,128]{2,1,0:T(8,128)S(1)} %get-tuple-element.64), custom_call_target="InvertDiagBlocksLowerTriangular" | custom-call | tf_op jit(solution)/shard_map/jit(cholesky)/cholesky | solution.py:67
  310.1 11.9 %cholesky.305 = f32[128,128]{1,0:T(8,128)S(1)} custom-call(f32[128,128]{1,0:T(8,128)S(1)} %cholesky.430), custom_call_target="Cholesky" | custom-call | tf_op jit(solution)/shard_map/jit(cholesky)/cholesky | solution.py:67
  322.0 9.8 %custom-call.32 = f32[1,128,128]{1,2,0:T(8,128)S(1)} custom-call(f32[1,128,128]{2,1,0:T(8,128)S(1)} %get-tuple-element.61), custom_call_target="InvertDiagBlocksLowerTriangular" | custom-call | tf_op jit(solution)/shard_map/jit(cholesky)/cholesky | solution.py:67
  332.5 11.7 %cholesky.326 = f32[128,128]{1,0:T(8,128)S(1)} custom-call(f32[128,128]{1,0:T(8,128)S(1)} %cholesky.435), custom_call_target="Cholesky" | custom-call | tf_op jit(solution)/shard_map/jit(cholesky)/cholesky | solution.py:67
  344.9 9.8 %custom-call.33 = f32[1,128,128]{1,2,0:T(8,128)S(1)} custom-call(f32[1,128,128]{2,1,0:T(8,128)S(1)} %get-tuple-element.58), custom_call_target="InvertDiagBlocksLowerTriangular" | custom-call | tf_op jit(solution)/shard_map/jit(cholesky)/cholesky | solution.py:67
  355.3 11.9 %cholesky.343 = f32[128,128]{1,0:T(8,128)S(1)} custom-call(f32[128,128]{1,0:T(8,128)S(1)} %convolution_subtract_fusion.8), custom_call_target="Cholesky" | custom-call | tf_op jit(solution)/shard_map/jit(cholesky)/cholesky | solution.py:67
  371.3 8.0 %while.2 = (s32[]{:T(128)}, f32[512,512]{1,0:T(8,128)S(1)}, s32[4,2]{0,1:T(2,128)S(1)}, f32[4,128,128]{2,1,0:T(8,128)S(1)}, s32[]{:T(128)}) while((s32[]{:T(128)}, f32[512,512]{1,0:T(8,128)S(1)}, s32[4,2]{0,1:T(2,128)S(1)}, f32[4,128,128]{2,1,0:T(8,128)S(1)}, s32[]{:T(128)}) %tuple.57), condition=%wide.while_cond, body=%wide.while_body.sunk | while | flops 2 | bytes 131181 | solution.py:68
  379.3 39.3 %custom-call.26 = f32[4,128,128]{1,2,0:T(8,128)S(1)} custom-call(f32[4,128,128]{2,1,0:T(8,128)S(1)} %get-tuple-element.14), custom_call_target="InvertDiagBlocksLowerTriangular" | custom-call | tf_op jit(solution)/shard_map/triangular_solve | solution.py:68
  420.2 5.3 fusion.81
  425.6 5.8 all-to-all-start.2
  439.6 12.5 %cholesky.358 = f32[128,128]{1,0:T(8,128)S(1)} custom-call(f32[128,128]{1,0:T(8,128)} %cholesky.439), custom_call_target="Cholesky" | custom-call | tf_op jit(solution)/shard_map/jit(cholesky)/cholesky | solution.py:67
  452.8 11.3 %custom-call.34 = f32[1,128,128]{1,2,0:T(8,128)} custom-call(f32[1,128,128]{2,1,0:T(8,128)} %get-tuple-element.54), custom_call_target="InvertDiagBlocksLowerTriangular" | custom-call | tf_op jit(solution)/shard_map/jit(cholesky)/cholesky | solution.py:67
  469.7 12.5 %cholesky.377 = f32[128,128]{1,0:T(8,128)S(1)} custom-call(f32[128,128]{1,0:T(8,128)} %cholesky.443), custom_call_target="Cholesky" | custom-call | tf_op jit(solution)/shard_map/jit(cholesky)/cholesky | solution.py:67
  482.9 10.8 %custom-call.35 = f32[1,128,128]{1,2,0:T(8,128)S(1)} custom-call(f32[1,128,128]{2,1,0:T(8,128)} %get-tuple-element.51), custom_call_target="InvertDiagBlocksLowerTriangular" | custom-call | tf_op jit(solution)/shard_map/jit(cholesky)/cholesky | solution.py:67
  498.3 12.5 %cholesky.398 = f32[128,128]{1,0:T(8,128)S(1)} custom-call(f32[128,128]{1,0:T(8,128)} %cholesky.448), custom_call_target="Cholesky" | custom-call | tf_op jit(solution)/shard_map/jit(cholesky)/cholesky | solution.py:67
  511.5 10.6 %custom-call.36 = f32[1,128,128]{1,2,0:T(8,128)S(1)} custom-call(f32[1,128,128]{2,1,0:T(8,128)} %get-tuple-element.48), custom_call_target="InvertDiagBlocksLowerTriangular" | custom-call | tf_op jit(solution)/shard_map/jit(cholesky)/cholesky | solution.py:67
  526.8 4.8 all-to-all-start.3
  532.5 12.5 %cholesky.415 = f32[128,128]{1,0:T(8,128)S(1)} custom-call(f32[128,128]{1,0:T(8,128)} %convolution_subtract_fusion.7), custom_call_target="Cholesky" | custom-call | tf_op jit(solution)/shard_map/jit(cholesky)/cholesky | solution.py:67
  551.9 8.0 %while.3 = (s32[]{:T(128)}, f32[512,512]{1,0:T(8,128)S(1)}, s32[4,2]{0,1:T(2,128)S(1)}, f32[4,128,128]{2,1,0:T(8,128)S(1)}, s32[]{:T(128)}) while((s32[]{:T(128)}, f32[512,512]{1,0:T(8,128)S(1)}, s32[4,2]{0,1:T(2,128)S(1)}, f32[4,128,128]{2,1,0:T(8,128)S(1)}, s32[]{:T(128)}) %tuple.69), condition=%wide.while_cond.1, body=%wide.while_body.1.sunk | while | flops 2 | bytes 131181 | solution.py:68
  559.9 39.3 %custom-call.27 = f32[4,128,128]{1,2,0:T(8,128)S(1)} custom-call(f32[4,128,128]{2,1,0:T(8,128)S(1)} %get-tuple-element.22), custom_call_target="InvertDiagBlocksLowerTriangular" | custom-call | tf_op jit(solution)/shard_map/triangular_solve | solution.py:68
  602.4 31.5 %all_to_all.30 = f32[32,16,192]{2,1,0:T(8,128)S(1)} all-to-all(f32[32,16,192]{2,1,0:T(8,128)S(1)} %bitcast.117), channel_id=1, replica_groups=mesh['row'=32,'col'=8] {'row'}, dimensions={0} | all-to-all | bytes 786432 | tf_op jit(solution)/shard_map/all_to_all | solution.py:30
  634.0 8.8 %all_to_all.31 = f32[8,16,1]{1,2,0:T(1,128)S(1)} all-to-all(f32[8,16,1]{1,2,0:T(1,128)S(1)} %broadcast_in_dim.12), channel_id=1, replica_groups=mesh['row'=32,'col'=8] {'col'}, dimensions={0} | all-to-all | bytes 1024 | tf_op jit(solution)/shard_map/all_to_all | solution.py:13
  643.1 49.0 %all_gather.15 = f32[512,193]{1,0:T(8,128)S(1)} all-gather(f32[16,193]{1,0:T(8,128)S(1)} %pad_maximum_fusion.10), channel_id=1, replica_groups=mesh['row'=32,'col'=8] {'row'}, dimensions={0}, use_global_device_ids=true | all-gather | bytes 407616 | tf_op jit(solution)/shard_map/all_gather | solution.py:37
  (169 shorter events, 84.1 us)
Async XLA Ops:
  7.2 86.4 %all-gather.3.cloned.1.call-start = ((), (), s32[]{:S(2)}) async-start(), calls=%async_computation.6 | async-start | bytes 3244032 | tf_op jit(solution)/shard_map/all_gather | solution.py:52
  64.9 28.7 %copy-start.4 = (f32[48,1536]{1,0:T(8,128)S(1)}, f32[48,1536]{1,0:T(8,128)}, u32[]{:S(2)}) copy-start(f32[48,1536]{1,0:T(8,128)} %param.8) | copy-start | bytes 884740
  64.9 28.7 %copy-start.5 = (f32[48,1536]{1,0:T(8,128)S(1)}, f32[48,1536]{1,0:T(8,128)}, u32[]{:S(2)}) copy-start(f32[48,1536]{1,0:T(8,128)} %param.7) | copy-start | bytes 884740
  64.9 47.7 %all-to-all-start.1 = ((f32[8,224,512]{2,1,0:T(8,128)}), f32[8,224,512]{2,1,0:T(8,128)}, u32[]{:S(2)}, u32[]{:S(2)}) async-start(f32[8,224,512]{2,1,0:T(8,128)} %broadcast_in_dim.10), calls=%async_computation.1 | async-start | bytes 7340032 | tf_op jit(solution)/shard_map/all_to_all | solution.py:13
  113.5 16.6 %all-to-all-start = ((f32[8,48,512]{2,1,0:T(8,128)}), f32[8,48,512]{2,1,0:T(8,128)S(1)}, u32[]{:S(2)}, u32[]{:S(2)}) async-start(f32[8,48,512]{2,1,0:T(8,128)} %broadcast_in_dim.8), calls=%async_computation | async-start | bytes 1572864 | tf_op jit(solution)/shard_map/all_to_all | solution.py:13
  118.4 165.9 %all-reduce.3.cloned.1.call-start = ((), (), s32[]{:S(2)}) async-start(), calls=%async_computation.7 | async-start | bytes 4194304 | tf_op jit(solution)/shard_map/psum | solution.py:45
  121.5 10.1 %copy-start.1 = (f32[224,512]{1,0:T(8,128)}, f32[224,512]{1,0:T(8,128)S(1)}, u32[]{:S(2)}) copy-start(f32[224,512]{1,0:T(8,128)S(1)} %reduce_sum.73) | copy-start | bytes 1376260
  418.8 6.7 copy-start.9
  419.2 6.3 copy-start.11
  419.7 5.9 copy-start.14
  420.2 5.3 copy-start.17
  425.6 100.3 %all-to-all-start.2 = ((f32[32,16,1536]{2,1,0:T(8,128)}), f32[32,16,1536]{2,1,0:T(8,128)S(1)}, u32[]{:S(2)}, u32[]{:S(2)}) async-start(f32[32,16,1536]{2,1,0:T(8,128)} %bitcast.114), calls=%async_computation.2 | async-start | bytes 6291456 | tf_op jit(solution)/shard_map/all_to_all | solution.py:30
  438.0 1.0 copy-start.3
  468.4 0.7 copy-start.13
  497.0 0.7 copy-start.16
  526.0 73.2 %copy-start.2 = (f32[224,512]{1,0:T(8,128)S(1)}, f32[224,512]{1,0:T(8,128)}, u32[]{:S(2)}) copy-start(f32[224,512]{1,0:T(8,128)} %copy-done.1) | copy-start | bytes 1376260
  526.8 19.5 %all-to-all-start.3 = ((f32[8,16,1]{1,2,0:T(1,128)}), f32[8,16,1]{1,2,0:T(1,128)S(1)}, u32[]{:S(2)}, u32[]{:S(2)}) async-start(f32[8,16,1]{1,2,0:T(1,128)} %broadcast_in_dim.11), calls=%async_computation.3 | async-start | bytes 8192 | tf_op jit(solution)/shard_map/all_to_all | solution.py:13
  531.6 164.2 %all-gather.5.cloned.1.call-start = ((), (), s32[]{:S(2)}) async-start(), calls=%async_computation.8 | async-start | bytes 3514368 | tf_op jit(solution)/shard_map/all_gather | solution.py:37
  546.5 54.6 %copy-start.19 = (f32[16,1536]{1,0:T(8,128)}, f32[16,1536]{1,0:T(8,128)S(1)}, u32[]{:S(2)}) copy-start(f32[16,1536]{1,0:T(8,128)S(1)} %broadcast_divide_fusion) | copy-start | bytes 294916
  547.2 54.1 %copy-start.7 = (f32[224,192]{0,1:T(8,128)S(1)}, f32[224,192]{0,1:T(8,128)}, u32[]{:S(2)}) copy-start(f32[224,192]{0,1:T(8,128)} %param.11) | copy-start | bytes 516100
  547.2 54.1 %copy-start.8 = (f32[224,192]{0,1:T(8,128)S(1)}, f32[224,192]{0,1:T(8,128)}, u32[]{:S(2)}) copy-start(f32[224,192]{0,1:T(8,128)} %param.10) | copy-start | bytes 516100
  601.3 94.4 %copy-start.10 = (f32[48,128]{1,0:T(8,128)S(1)}, f32[48,128]{1,0:T(8,128)}, u32[]{:S(2)}) copy-start(f32[48,128]{1,0:T(8,128)} %copy-done.9) | copy-start | bytes 73732
  601.4 94.4 %copy-start.12 = (f32[48,128]{1,0:T(8,128)S(1)}, f32[48,128]{1,0:T(8,128)}, u32[]{:S(2)}) copy-start(f32[48,128]{1,0:T(8,128)} %copy-done.11) | copy-start | bytes 73732
  601.4 94.4 %copy-start.15 = (f32[48,128]{1,0:T(8,128)S(1)}, f32[48,128]{1,0:T(8,128)}, u32[]{:S(2)}) copy-start(f32[48,128]{1,0:T(8,128)} %copy-done.14) | copy-start | bytes 73732
  601.4 94.4 %copy-start.18 = (f32[48,128]{1,0:T(8,128)S(1)}, f32[48,128]{1,0:T(8,128)}, u32[]{:S(2)}) copy-start(f32[48,128]{1,0:T(8,128)} %copy-done.17) | copy-start | bytes 73732
  643.0 57.5 %copy-start.20 = (f32[16,192]{1,0:T(8,128)}, f32[16,192]{1,0:T(8,128)S(1)}, u32[]{:S(2)}) copy-start(f32[16,192]{1,0:T(8,128)S(1)} %broadcast_divide_fusion.1) | copy-start | bytes 36868
  692.3 9.2 %copy-start.6 = (f32[48,1536]{1,0:T(8,128)S(1)}, f32[48,1536]{1,0:T(8,128)}, u32[]{:S(2)}) copy-start(f32[48,1536]{1,0:T(8,128)} %param.7) | copy-start | bytes 884740
  695.8 5.8 copy-start
Sparse Core Ops, SparseCore 0:
  10.6 82.9 all-gather.2
  133.1 151.1 all-reduce.2
  547.3 89.6 all-gather.4
where the time goes:
time: 717 us; the launch traced here: 711 us
  other arithmetic  254 us (35%)
  waiting for transfers between devices  197 us (27%)
  blocking collectives  142 us (20%)
  matrix products  41.9 us (6%)
  local copies, waits for them, and re-layouts  35.4 us (5%)
  starting transfers between devices  21.2 us (3%)
  between operations  19.9 us (3%)
    another operation x28, other arithmetic, finish(): lower = jnp.linalg.cholesky(gram)  166 us
    psum x1, waiting for transfers between devices, together(): so_far = lax.psum(jnp.concatenate([a.ravel() for a in arrays]), axis)  151 us
    another operation x5, other arithmetic, finish(): lax.linalg.triangular_solve(lower, proj, left_side=False, lower=True, tra...  80.1 us
    all_gather x1, blocking collectives, project(): lax.all_gather(basis, 'row', axis=0, tiled=True)  52.6 us
    all_gather x1, blocking collectives, in_one_piece(): whole = lax.all_gather(both, axis, axis=dim, tiled=True)  49 us
    all_to_all x1, blocking collectives, summed_on_arrival(): parts = lax.all_to_all(split_up(array, dim, size), axis, 0, 0, tiled=True)  31.5 us
    all_gather x1, waiting for transfers between devices, project(): lax.all_gather(basis, 'row', axis=0, tiled=True)  23.7 us
    all_to_all x3, waiting for transfers between devices, sent_to_all(): lax.all_to_all(jnp.broadcast_to(array[None], (size, *array.shape)), axis,...  21.4 us
  transfers between devices with their start and end apart: 7, of which 4 were waited for; matrix products, arithmetic and copies ran while one was open for 25% of the time, Pallas kernels for 0%

commit v1 on v0

--- a/solution.py
+++ b/solution.py
@@ -49,7 +49,12 @@
 def project(buffer, basis):
     partial_proj = jnp.dot(
         buffer,
-        lax.all_gather(basis, "row", axis=0, tiled=True).T,
+        jnp.concatenate(
+            lax.all_to_all(
+                jnp.stack([basis for _ in range(lax.axis_size("row"))], axis=0), "row", 0, 0
+            ),
+            axis=0,
+        ).T,
         precision=lax.Precision.HIGHEST,
         preferred_element_type=jnp.float32,
     )

time: 717 us -> 774 us (1.079)
  waiting for transfers between devices: 197 us -> 267 us
  blocking collectives: 142 us -> 117 us
    all_to_all x0 -> x1, waiting for transfers between devices: none -> 71.1 us  [project(): lax.all_to_all(jnp.stack([basis for _ in range(lax.axis_size('row'))], ax...]
    all_gather x1 -> x0, blocking collectives: 52.6 us -> none  [project(): lax.all_gather(basis, 'row', axis=0, tiled=True)]
    all_to_all x0 -> x1, blocking collectives: none -> 28.1 us  [project(): lax.all_to_all(jnp.stack([basis for _ in range(lax.axis_size('row'))], ax...]
    all_to_all x3, waiting for transfers between devices: 21.4 us -> 46 us  [sent_to_all(): lax.all_to_all(jnp.broadcast_to(array[None], (size, *array.shape)), axis,...]
    all_gather x1 -> x0, waiting for transfers between devices: 23.7 us -> none  [project(): lax.all_gather(basis, 'row', axis=0, tiled=True)]
    another operation x24 -> x26, local copies, waits for them, and re-layouts: 15.8 us -> 19.5 us
  transfers between devices with their start and end apart: 7 -> 7, of which waited for: 4 -> 4; matrix products, arithmetic and copies ran while one was open for 25% -> 23% of each run, Pallas kernels for 0% -> 0%
where the time goes in v1:
time: 774 us; the launch traced here: 768 us
  waiting for transfers between devices  267 us (34%)
  other arithmetic  254 us (33%)
  blocking collectives  117 us (15%)
  matrix products  41.8 us (5%)
  local copies, waits for them, and re-layouts  40.2 us (5%)
  starting transfers between devices  27 us (3%)
  between operations  20.2 us (3%)
    another operation x28, other arithmetic, finish(): lower = jnp.linalg.cholesky(gram)  166 us
    psum x1, waiting for transfers between devices, together(): so_far = lax.psum(jnp.concatenate([a.ravel() for a in arrays]), axis)  150 us
    another operation x5, other arithmetic, finish(): lax.linalg.triangular_solve(lower, proj, left_side=False, lower=True, tra...  80.1 us
    all_to_all x1, waiting for transfers between devices, project(): lax.all_to_all(jnp.stack([basis for _ in range(lax.axis_size('row'))], ax...  71.1 us
    all_gather x1, blocking collectives, in_one_piece(): whole = lax.all_gather(both, axis, axis=dim, tiled=True)  49 us
    all_to_all x3, waiting for transfers between devices, sent_to_all(): lax.all_to_all(jnp.broadcast_to(array[None], (size, *array.shape)), axis,...  46 us
    all_to_all x1, blocking collectives, summed_on_arrival(): parts = lax.all_to_all(split_up(array, dim, size), axis, 0, 0, tiled=True)  31.7 us
    all_to_all x1, blocking collectives, project(): lax.all_to_all(jnp.stack([basis for _ in range(lax.axis_size('row'))], ax...  28.1 us
  transfers between devices with their start and end apart: 7, of which 4 were waited for; matrix products, arithmetic and copies ran while one was open for 23% of the time, Pallas kernels for 0%

profile of v1, /device:TPU:8, one launch (start us, length us, event | category | flops | bytes accessed | tf_op | source)
XLA Modules:
  0.0 767.6 jit_solution(11073341572894060549)
XLA Ops:
  7.9 28.1 %all_to_all.40 = f32[32,16,192]{2,1,0:T(8,128)} all-to-all(f32[32,16,192]{2,1,0:T(8,128)S(1)} %stack.5), channel_id=1, replica_groups=mesh['row'=32,'col'=8] {'row'}, dimensions={0} | all-to-all | bytes 786432 | tf_op jit(solution)/shard_map/all_to_all | solution.py:53
  38.9 5.7 all-to-all-start
  47.5 71.1 %all-to-all-done = f32[32,16,1536]{2,1,0:T(8,128)S(1)} async-done(((f32[32,16,1536]{2,1,0:T(8,128)}), f32[32,16,1536]{2,1,0:T(8,128)S(1)}, u32[]{:S(2)}, u32[]{:S(2)}) %all-to-all-start) | async-done | bytes 3145760 | tf_op jit(solution)/shard_map/all_to_all | solution.py:53
  121.9 5.0 all-to-all-start.3
  131.0 38.7 %all-to-all-done.3 = f32[8,224,512]{2,1,0:T(8,128)} async-done(((f32[8,224,512]{2,1,0:T(8,128)}), f32[8,224,512]{2,1,0:T(8,128)}, u32[]{:S(2)}, u32[]{:S(2)}) %all-to-all-start.3) | async-done | bytes 3670048 | tf_op jit(solution)/shard_map/all_to_all | solution.py:13
  170.7 4.9 all-to-all-start.1
  180.0 7.3 all-to-all-done.1
  190.2 150.2 %all-reduce.3.cloned.1.call-done = f32[524288]{0:T(1024)} async-done(((f32[524288]{0:T(1024)}), f32[524288]{0:T(1024)}) %all-reduce.3.cloned.1.call-update) | async-done | bytes 2097168 | tf_op jit(solution)/shard_map/psum | solution.py:45
  343.8 11.7 %cholesky.286 = f32[128,128]{1,0:T(8,128)S(1)} custom-call(f32[128,128]{1,0:T(8,128)S(1)} %cholesky.426), custom_call_target="Cholesky" | custom-call | tf_op jit(solution)/shard_map/jit(cholesky)/cholesky | solution.py:72
  355.5 9.8 %custom-call.31 = f32[1,128,128]{1,2,0:T(8,128)S(1)} custom-call(f32[1,128,128]{2,1,0:T(8,128)S(1)} %get-tuple-element.64), custom_call_target="InvertDiagBlocksLowerTriangular" | custom-call | tf_op jit(solution)/shard_map/jit(cholesky)/cholesky | solution.py:72
  366.1 11.9 %cholesky.305 = f32[128,128]{1,0:T(8,128)S(1)} custom-call(f32[128,128]{1,0:T(8,128)S(1)} %cholesky.430), custom_call_target="Cholesky" | custom-call | tf_op jit(solution)/shard_map/jit(cholesky)/cholesky | solution.py:72
  378.0 9.8 %custom-call.32 = f32[1,128,128]{1,2,0:T(8,128)S(1)} custom-call(f32[1,128,128]{2,1,0:T(8,128)S(1)} %get-tuple-element.61), custom_call_target="InvertDiagBlocksLowerTriangular" | custom-call | tf_op jit(solution)/shard_map/jit(cholesky)/cholesky | solution.py:72
  388.5 11.7 %cholesky.326 = f32[128,128]{1,0:T(8,128)S(1)} custom-call(f32[128,128]{1,0:T(8,128)S(1)} %cholesky.435), custom_call_target="Cholesky" | custom-call | tf_op jit(solution)/shard_map/jit(cholesky)/cholesky | solution.py:72
  400.9 9.8 %custom-call.33 = f32[1,128,128]{1,2,0:T(8,128)S(1)} custom-call(f32[1,128,128]{2,1,0:T(8,128)S(1)} %get-tuple-element.58), custom_call_target="InvertDiagBlocksLowerTriangular" | custom-call | tf_op jit(solution)/shard_map/jit(cholesky)/cholesky | solution.py:72
  411.3 11.9 %cholesky.343 = f32[128,128]{1,0:T(8,128)S(1)} custom-call(f32[128,128]{1,0:T(8,128)S(1)} %convolution_subtract_fusion.8), custom_call_target="Cholesky" | custom-call | tf_op jit(solution)/shard_map/jit(cholesky)/cholesky | solution.py:72
  427.3 8.0 %while.2 = (s32[]{:T(128)}, f32[512,512]{1,0:T(8,128)S(1)}, s32[4,2]{0,1:T(2,128)S(1)}, f32[4,128,128]{2,1,0:T(8,128)S(1)}, s32[]{:T(128)}) while((s32[]{:T(128)}, f32[512,512]{1,0:T(8,128)S(1)}, s32[4,2]{0,1:T(2,128)S(1)}, f32[4,128,128]{2,1,0:T(8,128)S(1)}, s32[]{:T(128)}) %tuple.57), condition=%wide.while_cond, body=%wide.while_body.sunk | while | flops 2 | bytes 131181 | solution.py:73
  435.3 39.3 %custom-call.26 = f32[4,128,128]{1,2,0:T(8,128)S(1)} custom-call(f32[4,128,128]{2,1,0:T(8,128)S(1)} %get-tuple-element.14), custom_call_target="InvertDiagBlocksLowerTriangular" | custom-call | tf_op jit(solution)/shard_map/triangular_solve | solution.py:73
  476.3 5.3 fusion.81
  481.6 5.8 all-to-all-start.4
  495.7 12.5 %cholesky.358 = f32[128,128]{1,0:T(8,128)S(1)} custom-call(f32[128,128]{1,0:T(8,128)} %cholesky.439), custom_call_target="Cholesky" | custom-call | tf_op jit(solution)/shard_map/jit(cholesky)/cholesky | solution.py:72
  508.9 11.3 %custom-call.34 = f32[1,128,128]{1,2,0:T(8,128)} custom-call(f32[1,128,128]{2,1,0:T(8,128)} %get-tuple-element.54), custom_call_target="InvertDiagBlocksLowerTriangular" | custom-call | tf_op jit(solution)/shard_map/jit(cholesky)/cholesky | solution.py:72
  525.8 12.5 %cholesky.377 = f32[128,128]{1,0:T(8,128)S(1)} custom-call(f32[128,128]{1,0:T(8,128)} %cholesky.443), custom_call_target="Cholesky" | custom-call | tf_op jit(solution)/shard_map/jit(cholesky)/cholesky | solution.py:72
  539.0 10.8 %custom-call.35 = f32[1,128,128]{1,2,0:T(8,128)S(1)} custom-call(f32[1,128,128]{2,1,0:T(8,128)} %get-tuple-element.51), custom_call_target="InvertDiagBlocksLowerTriangular" | custom-call | tf_op jit(solution)/shard_map/jit(cholesky)/cholesky | solution.py:72
  554.4 12.5 %cholesky.398 = f32[128,128]{1,0:T(8,128)S(1)} custom-call(f32[128,128]{1,0:T(8,128)} %cholesky.448), custom_call_target="Cholesky" | custom-call | tf_op jit(solution)/shard_map/jit(cholesky)/cholesky | solution.py:72
  567.6 10.6 %custom-call.36 = f32[1,128,128]{1,2,0:T(8,128)S(1)} custom-call(f32[1,128,128]{2,1,0:T(8,128)} %get-tuple-element.48), custom_call_target="InvertDiagBlocksLowerTriangular" | custom-call | tf_op jit(solution)/shard_map/jit(cholesky)/cholesky | solution.py:72
  582.8 4.8 all-to-all-start.5
  588.5 12.5 %cholesky.415 = f32[128,128]{1,0:T(8,128)S(1)} custom-call(f32[128,128]{1,0:T(8,128)} %convolution_subtract_fusion.7), custom_call_target="Cholesky" | custom-call | tf_op jit(solution)/shard_map/jit(cholesky)/cholesky | solution.py:72
  607.9 8.0 %while.3 = (s32[]{:T(128)}, f32[512,512]{1,0:T(8,128)S(1)}, s32[4,2]{0,1:T(2,128)S(1)}, f32[4,128,128]{2,1,0:T(8,128)S(1)}, s32[]{:T(128)}) while((s32[]{:T(128)}, f32[512,512]{1,0:T(8,128)S(1)}, s32[4,2]{0,1:T(2,128)S(1)}, f32[4,128,128]{2,1,0:T(8,128)S(1)}, s32[]{:T(128)}) %tuple.67), condition=%wide.while_cond.1, body=%wide.while_body.1.sunk | while | flops 2 | bytes 131181 | solution.py:73
  616.0 39.3 %custom-call.27 = f32[4,128,128]{1,2,0:T(8,128)S(1)} custom-call(f32[4,128,128]{2,1,0:T(8,128)S(1)} %get-tuple-element.22), custom_call_target="InvertDiagBlocksLowerTriangular" | custom-call | tf_op jit(solution)/shard_map/triangular_solve | solution.py:73
  658.5 31.7 %all_to_all.41 = f32[32,16,192]{2,1,0:T(8,128)S(1)} all-to-all(f32[32,16,192]{2,1,0:T(8,128)S(1)} %bitcast.121), channel_id=1, replica_groups=mesh['row'=32,'col'=8] {'row'}, dimensions={0} | all-to-all | bytes 786432 | tf_op jit(solution)/shard_map/all_to_all | solution.py:30
  690.3 8.5 %all_to_all.42 = f32[8,16,1]{1,2,0:T(1,128)S(1)} all-to-all(f32[8,16,1]{1,2,0:T(1,128)S(1)} %broadcast_in_dim.12), channel_id=1, replica_groups=mesh['row'=32,'col'=8] {'col'}, dimensions={0} | all-to-all | bytes 1024 | tf_op jit(solution)/shard_map/all_to_all | solution.py:13
  699.1 49.0 %all_gather.7 = f32[512,193]{1,0:T(8,128)S(1)} all-gather(f32[16,193]{1,0:T(8,128)S(1)} %pad_maximum_fusion.10), channel_id=1, replica_groups=mesh['row'=32,'col'=8] {'row'}, dimensions={0}, use_global_device_ids=true | all-gather | bytes 407616 | tf_op jit(solution)/shard_map/all_gather | solution.py:37
  (172 shorter events, 93.0 us)
Async XLA Ops:
  38.9 5.8 copy-start.6
  38.9 5.8 copy-start.8
  38.9 79.7 %all-to-all-start = ((f32[32,16,1536]{2,1,0:T(8,128)}), f32[32,16,1536]{2,1,0:T(8,128)S(1)}, u32[]{:S(2)}, u32[]{:S(2)}) async-start(f32[32,16,1536]{2,1,0:T(8,128)} %stack.4), calls=%async_computation | async-start | bytes 6291456 | tf_op jit(solution)/shard_map/all_to_all | solution.py:53
  121.9 5.1 copy-start.4
  121.9 47.8 %all-to-all-start.3 = ((f32[8,224,512]{2,1,0:T(8,128)}), f32[8,224,512]{2,1,0:T(8,128)}, u32[]{:S(2)}, u32[]{:S(2)}) async-start(f32[8,224,512]{2,1,0:T(8,128)} %broadcast_in_dim.10), calls=%async_computation.3 | async-start | bytes 7340032 | tf_op jit(solution)/shard_map/all_to_all | solution.py:13
  170.7 16.6 %all-to-all-start.1 = ((f32[8,48,512]{2,1,0:T(8,128)}), f32[8,48,512]{2,1,0:T(8,128)S(1)}, u32[]{:S(2)}, u32[]{:S(2)}) async-start(f32[8,48,512]{2,1,0:T(8,128)} %broadcast_in_dim.8), calls=%async_computation.1 | async-start | bytes 1572864 | tf_op jit(solution)/shard_map/all_to_all | solution.py:13
  175.6 164.8 %all-reduce.3.cloned.1.call-start = ((), (), s32[]{:S(2)}) async-start(), calls=%async_computation.8 | async-start | bytes 4194304 | tf_op jit(solution)/shard_map/psum | solution.py:45
  178.6 10.1 %copy-start.1 = (f32[224,512]{1,0:T(8,128)}, f32[224,512]{1,0:T(8,128)S(1)}, u32[]{:S(2)}) copy-start(f32[224,512]{1,0:T(8,128)S(1)} %reduce_sum.73) | copy-start | bytes 1376260
  474.8 6.7 copy-start.10
  475.3 6.3 copy-start.12
  475.7 5.8 copy-start.15
  476.3 5.3 copy-start.18
  481.6 100.4 %all-to-all-start.4 = ((f32[32,16,1536]{2,1,0:T(8,128)}), f32[32,16,1536]{2,1,0:T(8,128)S(1)}, u32[]{:S(2)}, u32[]{:S(2)}) async-start(f32[32,16,1536]{2,1,0:T(8,128)} %bitcast.116), calls=%async_computation.4 | async-start | bytes 6291456 | tf_op jit(solution)/shard_map/all_to_all | solution.py:30
  494.1 1.0 copy-start.3
  524.5 0.7 copy-start.14
  553.1 0.7 copy-start.17
  582.1 73.2 %copy-start.2 = (f32[224,512]{1,0:T(8,128)S(1)}, f32[224,512]{1,0:T(8,128)}, u32[]{:S(2)}) copy-start(f32[224,512]{1,0:T(8,128)} %copy-done.1) | copy-start | bytes 1376260
  582.8 19.5 %all-to-all-start.5 = ((f32[8,16,1]{1,2,0:T(1,128)}), f32[8,16,1]{1,2,0:T(1,128)S(1)}, u32[]{:S(2)}, u32[]{:S(2)}) async-start(f32[8,16,1]{1,2,0:T(1,128)} %broadcast_in_dim.11), calls=%async_computation.5 | async-start | bytes 8192 | tf_op jit(solution)/shard_map/all_to_all | solution.py:13
  587.7 164.1 %all-gather.2.cloned.1.call-start = ((), (), s32[]{:S(2)}) async-start(), calls=%async_computation.9 | async-start | bytes 3514368 | tf_op jit(solution)/shard_map/all_gather | solution.py:37
  602.5 54.6 %copy-start.20 = (f32[16,1536]{1,0:T(8,128)}, f32[16,1536]{1,0:T(8,128)S(1)}, u32[]{:S(2)}) copy-start(f32[16,1536]{1,0:T(8,128)S(1)} %broadcast_divide_fusion) | copy-start | bytes 294916
  603.3 54.1 %copy-start.7 = (f32[224,192]{0,1:T(8,128)S(1)}, f32[224,192]{0,1:T(8,128)}, u32[]{:S(2)}) copy-start(f32[224,192]{0,1:T(8,128)} %param.11) | copy-start | bytes 516100
  603.3 54.1 %copy-start.9 = (f32[224,192]{0,1:T(8,128)S(1)}, f32[224,192]{0,1:T(8,128)}, u32[]{:S(2)}) copy-start(f32[224,192]{0,1:T(8,128)} %param.10) | copy-start | bytes 516100
  657.4 94.4 %copy-start.11 = (f32[48,128]{1,0:T(8,128)S(1)}, f32[48,128]{1,0:T(8,128)}, u32[]{:S(2)}) copy-start(f32[48,128]{1,0:T(8,128)} %copy-done.10) | copy-start | bytes 73732
  657.4 94.4 %copy-start.13 = (f32[48,128]{1,0:T(8,128)S(1)}, f32[48,128]{1,0:T(8,128)}, u32[]{:S(2)}) copy-start(f32[48,128]{1,0:T(8,128)} %copy-done.12) | copy-start | bytes 73732
  657.4 94.4 %copy-start.16 = (f32[48,128]{1,0:T(8,128)S(1)}, f32[48,128]{1,0:T(8,128)}, u32[]{:S(2)}) copy-start(f32[48,128]{1,0:T(8,128)} %copy-done.15) | copy-start | bytes 73732
  657.5 94.4 %copy-start.19 = (f32[48,128]{1,0:T(8,128)S(1)}, f32[48,128]{1,0:T(8,128)}, u32[]{:S(2)}) copy-start(f32[48,128]{1,0:T(8,128)} %copy-done.18) | copy-start | bytes 73732
  699.0 57.5 %copy-start.21 = (f32[16,192]{1,0:T(8,128)}, f32[16,192]{1,0:T(8,128)S(1)}, u32[]{:S(2)}) copy-start(f32[16,192]{1,0:T(8,128)S(1)} %broadcast_divide_fusion.1) | copy-start | bytes 36868
  748.4 9.2 %copy-start.5 = (f32[48,1536]{1,0:T(8,128)S(1)}, f32[48,1536]{1,0:T(8,128)}, u32[]{:S(2)}) copy-start(f32[48,1536]{1,0:T(8,128)} %param.7) | copy-start | bytes 884740
  751.8 5.8 copy-start
Sparse Core Ops, SparseCore 0:
  190.3 150.0 all-reduce.2
  603.4 89.4 all-gather.1
